TPU v7x, 32 devices: a whole 2x2x4 slice. The times are simulated.
32 devices in a mesh: row: 4 (over y, core), col: 8 (over z, x).
Axes of the slice: x: 2, y: 2, z: 4, core: 2. Of those that a mesh axis runs over, the one named last changes fastest.
Arguments:
- positions: float32 [3, 512], P(None, ('row', 'col')), as said below
- thermal_noise: float32 [32, 3, 512], P(None, None, ('row', 'col')), as said below
Outputs:
- displacement: float32 [32, 3, 512], P(None, None, ('row', 'col'))
Inputs may be any that keep to these rules, and one draw needn't show every extreme that they name: `positions`: any two particles are at least 1.0 apart. `thermal_noise`: finite real entries.
All inputs are finite; a program needn't handle non-finite values.
Results may differ from a plain program's by a relative error of at most 0.0013.
Values may be sent and summed in bfloat16 or wider, within the bound.
A program may use at most 64 MiB of HBM per device.

v0:
```python
import functools

import jax
import jax.numpy as jnp
from jax import lax
from jax.experimental import pallas as pl
from jax.experimental.pallas import tpu as pltpu
from jax.sharding import PartitionSpec as P

LANES = 128
MESH = pl.DeviceIdType.MESH
BLOCKS = ((0, 0), (1, 1), (2, 2), (0, 1), (0, 2), (1, 2))


def partner(place, k, size):
    result = 0
    bit = 1
    while bit < size:
        digit = lax.rem(place // bit, 2)
        result = result + bit * (1 - digit if k & bit else digit)
        bit = 2 * bit
    return result


def replicated_kernel(
    rows,
    outer,
    inner,
    noise_ref,
    pos_ref,
    out_ref,
    gathered,
    stage,
    own_ref,
    noise_full,
    pos_cols,
    pos_rows,
    mobility,
    weights,
    image,
    send_line,
    recv_line,
    send_plane,
    recv_plane,
):
    _, per_device, samples = noise_ref.shape
    particles = rows * outer * inner * per_device
    f32, bf16 = jnp.float32, jnp.bfloat16
    my_row, my_col = lax.axis_index("row"), lax.axis_index("col")

    my_outer, my_inner = my_col // inner, lax.rem(my_col, inner)
    line = [partner(my_outer, k, outer) for k in range(outer)]
    plane = [
        (partner(my_row, j, rows), partner(my_inner, i, inner))
        for i in range(inner)
        for j in range(rows)
    ]

    barrier = pltpu.get_barrier_semaphore()
    for place in line[1:]:
        pl.semaphore_signal(
            barrier, inc=1, device_id=(my_row, place * inner + my_inner), device_id_type=MESH
        )
    for row, place in plane[1:]:
        pl.semaphore_signal(
            barrier, inc=1, device_id=(row, my_outer * inner + place), device_id_type=MESH
        )

    stage[...] = jnp.zeros_like(stage)
    position = pos_ref[...]
    for term in range(3):
        piece = position.astype(bf16).astype(f32)
        stage[pl.ds(3 * term, 3), pl.ds(0, per_device)] = piece
        position = position - piece
    turned = jnp.transpose(stage[...])
    own_ref[...] = jnp.zeros_like(own_ref)
    for b in range(3):
        own_ref[:, pl.ds(b * samples, samples)] = noise_ref[b]
    own_ref[:, pl.ds(3 * samples, 16)] = turned[0:per_device, :]
    own = own_ref[...]
    gathered[0, 0] = own.astype(bf16)

    pl.semaphore_wait(barrier, len(line) + len(plane) - 2)

    def line_copy(k):
        return pltpu.make_async_remote_copy(
            src_ref=gathered.at[0, 0],
            dst_ref=gathered.at[0, k],
            send_sem=send_line.at[k],
            recv_sem=recv_line.at[k],
            device_id=(my_row, line[k] * inner + my_inner),
            device_id_type=MESH,
        )

    def plane_copy(block, k):
        return pltpu.make_async_remote_copy(
            src_ref=gathered.at[0, block],
            dst_ref=gathered.at[k, block],
            send_sem=send_plane.at[k],
            recv_sem=recv_plane.at[k],
            device_id=(plane[k][0], my_outer * inner + plane[k][1]),
            device_id_type=MESH,
        )

    def finished(ref, semaphore):
        pltpu.make_async_copy(ref, ref, semaphore).wait()

    for k in range(outer - 1, 0, -1):
        line_copy(k).start()
    for k in range(1, len(plane)):
        plane_copy(0, k).start()
    for block in range(1, outer):
        finished(gathered.at[0, block], recv_line.at[block])
        for k in range(1, len(plane)):
            plane_copy(block, k).start()

    lane = lax.broadcasted_iota(jnp.int32, (1, LANES), 1)
    field = lax.broadcasted_iota(jnp.int32, (LANES, 3 * LANES), 0) - 3 * samples
    target = lax.broadcasted_iota(jnp.int32, (LANES, 3 * LANES), 1) // LANES
    select = (field == target) | (field == target + 3) | (field == target + 6)
    over_lanes = select.astype(f32).astype(bf16)
    field = lax.broadcasted_iota(jnp.int32, (3 * 16, LANES), 1) - 3 * samples
    target = lax.broadcasted_iota(jnp.int32, (3 * 16, LANES), 0) // 16
    select = (field == target) | (field == target + 3) | (field == target + 6)
    over_rows = select.astype(f32).astype(bf16)
    tiles = particles // LANES

    def form(start, tile, on_diagonal):
        at_rows = pl.ds(start, 16)
        d = [
            pos_cols[at_rows, pl.ds(a * LANES, LANES)]
            - pos_rows[pl.ds(a * 16, 16), pl.ds(tile * LANES, LANES)]
            for a in range(3)
        ]
        q = d[0] * d[0] + d[1] * d[1] + d[2] * d[2]
        if on_diagonal:
            row_label = start + lax.broadcasted_iota(jnp.int32, (16, LANES), 0)
            col_label = tile * LANES + lax.broadcasted_iota(jnp.int32, (16, LANES), 1)
            retain = row_label != col_label
            q = jnp.where(retain, q, 4.0)
        u = lax.rsqrt(q)
        r = q * u
        near = r < 2.0
        u2 = u * u
        f = jnp.where(near, 1.0 - 0.28125 * r, u * (0.75 + 0.5 * u2))
        if on_diagonal:
            f = jnp.where(retain, f, 0.0)
        h = u * jnp.where(near, 0.09375, u2 * (0.75 - 1.5 * u2))
        hd = [h * d[a] for a in range(3)]
        for n, (a, b) in enumerate(BLOCKS):
            element = hd[a] * d[b]
            if a == b:
                element = element + f
            mobility[n * tiles + tile, at_rows, :] = element.astype(bf16)

    group = lane // samples

    def set_weights(start, x):
        down = pltpu.roll(x, LANES - samples, 1)
        up = pltpu.roll(x, samples, 1)
        across = pltpu.roll(x, 2 * samples, 1)
        moved = {
            (0, 0): jnp.where(group == 0, x, 0.0),
            (1, 1): jnp.where(group == 1, x, 0.0),
            (2, 2): jnp.where(group == 2, x, 0.0),
            (0, 1): jnp.where(group == 0, down, jnp.where(group == 1, up, 0.0)),
            (1, 2): jnp.where(group == 1, down, jnp.where(group == 2, up, 0.0)),
            (0, 2): jnp.where((group == 0) | (group == 2), across, 0.0),
        }
        for n, pair in enumerate(BLOCKS):
            weights[pl.ds(n * particles + start, x.shape[0]), :] = moved[pair].astype(bf16)

    def fold(x):
        return jnp.sum(x.reshape(-1, 8, LANES), axis=0)

    def total(x):
        row = jnp.broadcast_to(jnp.sum(x, axis=0, keepdims=True), (8, LANES))
        row = row + pltpu.roll(row, 2 * samples, 1)
        row = row + pltpu.roll(row, samples, 1)
        return row[0:1, :]

    step_rows = 64

    def sweep(function):
        def step(index, partial):
            start = index * step_rows
            return partial + function(start, pl.ds(start, step_rows))

        partial = jnp.zeros((8, LANES), f32)
        for index in range(particles // step_rows):
            partial = step(index, partial)
        return total(partial)

    def product(row_tiles, col_tiles):
        at_rows = pl.ds(row_tiles[0] * LANES, len(row_tiles) * LANES)
        first, count = col_tiles[0], len(col_tiles)
        left = jnp.concatenate(
            [mobility[n * tiles + first + t, at_rows, :] for n in range(6) for t in range(count)],
            axis=1,
        )
        right = jnp.concatenate(
            [
                weights[pl.ds(n * particles + first * LANES, count * LANES), :]
                for n in range(6)
            ],
            axis=0,
        )
        return jnp.dot(left, right, preferred_element_type=f32)

    is_noise = lane < 3 * samples
    at_own = pl.ds(0, per_device)
    low, high = list(range(tiles // 2)), list(range(tiles // 2, tiles))
    early, late = list(range(tiles // 2)), list(range(tiles // 2, tiles))
    at_low, at_high = pl.ds(0, particles // 2), pl.ds(particles // 2, particles // 2)
    at_early, at_late = pl.ds(0, len(early) * LANES), pl.ds(len(early) * LANES, len(late) * LANES)
    per_tile = LANES // (outer * per_device)
    for tile in range(tiles):
        for k in range(tile * per_tile, (tile + 1) * per_tile):
            if k:
                finished(gathered.at[k], recv_plane.at[k])
        packed = gathered[pl.ds(tile * per_tile, per_tile)].reshape(LANES, LANES)
        pos_cols[pl.ds(tile * LANES, LANES), :] = jnp.dot(
            packed, over_lanes, preferred_element_type=f32
        )
        pos_rows[:, pl.ds(tile * LANES, LANES)] = lax.dot_general(
            over_rows, packed, (((1,), (1,)), ((), ())), preferred_element_type=f32
        )

        wide = packed.astype(f32)
        noise_full[pl.ds(tile * LANES, LANES), :] = jnp.where(is_noise, wide, 0.0)
        set_weights(tile * LANES, wide)

        if tile == tiles - 1:
            image[pl.ds(0, len(early) * LANES), :] = product(early, low)
            for step in range(LANES // 16):
                for other in range(tile + 1):
                    form(tile * LANES + step * 16, other, other == tile)
                for other in range(tile):
                    form(other * LANES + step * 16, tile, False)
        else:

            @pl.loop(0, LANES // 16)
            def _(step, tile=tile):
                for other in range(tile + 1):
                    start = pl.multiple_of(tile * LANES + step * 16, 16)
                    form(start, other, other == tile)
                for other in range(tile):
                    start = pl.multiple_of(other * LANES + step * 16, 16)
                    form(start, tile, False)

    noise_full[at_own, :] = jnp.where(is_noise, own_ref[...], 0.0)

    def noise_square(start, at):
        return fold(noise_full[at, :] * noise_full[at, :])

    length = jnp.sqrt(sweep(noise_square) + 1e-06)
    inverse = 1.0 / length
    image[at_early, :] = image[at_early, :] + product(early, high)
    image[at_late, :] = product(late, low + high)

    def first_quotient(start, at):
        basis_one = noise_full[at, :] * inverse
        image_one = basis_one + image[at, :] * inverse
        noise_full[at, :] = basis_one
        image[at, :] = image_one
        return fold(basis_one * image_one)

    alpha_one = sweep(first_quotient)

    def remainder_square(start, at):
        remainder = image[at, :] - alpha_one * noise_full[at, :]
        image[at, :] = remainder
        return fold(remainder * remainder)

    beta_one = jnp.sqrt(sweep(remainder_square) + 1e-06)
    inverse_beta = 1.0 / beta_one

    def second_basis(start, at):
        basis_two = image[at, :] * inverse_beta
        image[at, :] = basis_two
        set_weights(start, basis_two)
        return fold(basis_two * basis_two)

    alpha_two = sweep(second_basis)
    alpha_two = alpha_two + total(
        fold(image[at_low, :] * product(low, low))
        + 2.0 * fold(image[at_low, :] * product(low, high))
        + fold(image[at_high, :] * product(high, high))
    )
    det_root = jnp.sqrt(alpha_one * alpha_two - beta_one * beta_one)
    trace_root = jnp.sqrt(alpha_one + alpha_two + 2.0 * det_root)
    weight_one = (alpha_one + det_root) / trace_root
    weight_two = beta_one / trace_root
    result = 0.5 * length * (weight_one * noise_full[at_own, :] + weight_two * image[at_own, :])
    for b in range(3):
        out_ref[b] = result[:, b * samples : (b + 1) * samples]

    for k in range(1, outer):
        line_copy(k).wait_send()
    for k in range(1, len(plane)):
        finished(gathered.at[0], send_plane.at[k])


def replicated(mesh, positions, thermal_noise):
    rows, cols = mesh.shape["row"], mesh.shape["col"]
    samples, _, per_device = thermal_noise.shape
    particles = rows * cols * per_device
    inner = 2 if cols % 2 == 0 else 1
    outer = cols // inner
    f32, bf16 = jnp.float32, jnp.bfloat16
    vmem = pl.BlockSpec(memory_space=pltpu.VMEM)
    out = pl.pallas_call(
        functools.partial(replicated_kernel, rows, outer, inner),
        out_shape=jax.ShapeDtypeStruct((3, per_device, samples), f32),
        in_specs=[vmem, vmem],
        out_specs=vmem,
        scratch_shapes=[
            pltpu.VMEM((rows * inner, outer, per_device, LANES), bf16),
            pltpu.VMEM((16, LANES), f32),
            pltpu.VMEM((per_device, LANES), f32),
            pltpu.VMEM((particles, LANES), f32),
            pltpu.VMEM((particles, 3 * LANES), f32),
            pltpu.VMEM((3 * 16, particles), f32),
            pltpu.VMEM((6 * particles // LANES, particles, LANES), bf16),
            pltpu.VMEM((6 * particles, LANES), bf16),
            pltpu.VMEM((particles, LANES), f32),
            pltpu.SemaphoreType.DMA((outer,)),
            pltpu.SemaphoreType.DMA((outer,)),
            pltpu.SemaphoreType.DMA((rows * inner,)),
            pltpu.SemaphoreType.DMA((rows * inner,)),
        ],
        compiler_params=pltpu.CompilerParams(collective_id=0, has_side_effects=True),
        name="lanczos",
    )(jnp.transpose(thermal_noise, (1, 2, 0)), positions)
    return jnp.transpose(out, (2, 0, 1))


def fits(mesh, positions, thermal_noise):
    rows, cols = mesh.shape["row"], mesh.shape["col"]
    samples, _, particles = thermal_noise.shape
    per_device = particles // (rows * cols)
    outer = cols // 2 if cols % 2 == 0 else cols
    return (
        rows & (rows - 1) == 0
        and cols & (cols - 1) == 0
        and 4 * samples == LANES
        and per_device % 16 == 0
        and LANES % (outer * per_device) == 0
        and particles % (2 * LANES) == 0
        and 12 * particles * particles <= 2**24
    )


def pair_tensor(rows_pos, cols_pos, retain):
    offsets = [rows_pos[a][None, :] - cols_pos[a][:, None] for a in range(3)]
    squared = offsets[0] * offsets[0] + offsets[1] * offsets[1] + offsets[2] * offsets[2]
    guarded = jnp.where(retain, squared, 4.0)
    inverse = lax.rsqrt(guarded)
    distance = guarded * inverse
    correlation = distance < 2.0
    inverse_cube = inverse * inverse * inverse
    inverse_fifth = inverse_cube * inverse * inverse
    isotropic = jnp.where(
        correlation, 1.0 - 0.28125 * distance, 0.75 * inverse + 0.5 * inverse_cube
    )
    dyadic = jnp.where(correlation, 0.09375 * inverse, 0.75 * inverse_cube - 1.5 * inverse_fifth)
    isotropic = jnp.where(retain, isotropic, 0.0)
    dyadic = jnp.where(retain, dyadic, 0.0)
    columns = []
    for b in range(3):
        elements = []
        for a in range(3):
            element = dyadic * offsets[a] * offsets[b]
            if a == b:
                element = element + isotropic
            elements.append(element)
        columns.append(jnp.stack(elements, axis=1))
    return jnp.stack(columns, axis=0)


def half_image(pos_rows, pos_cols, vec_rows, vec_cols, own_vector):
    row_devices = lax.axis_size("row")
    col_devices = lax.axis_size("col")
    row_index = lax.axis_index("row")
    col_index = lax.axis_index("col")
    samples = own_vector.shape[0]
    per_device = own_vector.shape[2]
    row_count = pos_rows.shape[1]
    row_label = row_index * col_devices * per_device + lax.iota(jnp.int32, row_count)
    group_size = min(row_devices, max(1, 128 // per_device))
    width = group_size * per_device
    group_count = row_devices // group_size
    sum_rows = jnp.zeros((samples, 3, row_count), jnp.float32)
    sum_cols = jnp.zeros((samples, 3, per_device * row_devices), jnp.float32)

    def add_group(group, totals):
        sum_rows, sum_cols = totals
        start = group * width
        cols_pos = lax.dynamic_slice_in_dim(pos_cols, start, width, 1)
        cols_vec = lax.dynamic_slice_in_dim(vec_cols, start, width, 2)
        local_cols = lax.iota(jnp.int32, width)
        segment = group * group_size + local_cols // per_device
        col_label = (segment * col_devices + col_index) * per_device + local_cols % per_device
        keep = segment >= row_index
        upper = (segment != row_index)[:, None] | (row_label[None, :] < col_label[:, None])
        retain = keep[:, None] & upper & (row_label[None, :] != col_label[:, None])
        tensor = pair_tensor(pos_rows, cols_pos, retain).astype(jnp.bfloat16)
        sum_rows = sum_rows + jnp.einsum(
            "kbj,bjai->kai", cols_vec, tensor, preferred_element_type=jnp.float32
        )
        credit = jnp.einsum("kai,bjai->kbj", vec_rows, tensor, preferred_element_type=jnp.float32)
        previous = lax.dynamic_slice_in_dim(sum_cols, start, width, 2)
        sum_cols = lax.dynamic_update_slice_in_dim(sum_cols, previous + credit, start, 2)
        return (sum_rows, sum_cols)

    totals = (sum_rows, sum_cols)
    totals = lax.fori_loop(row_index // group_size, group_count, add_group, totals)
    sum_rows, sum_cols = totals
    mobility_image = own_vector + lax.psum_scatter(sum_rows, "col", scatter_dimension=2, tiled=True)
    return mobility_image + lax.psum_scatter(sum_cols, "row", scatter_dimension=2, tiled=True)


def on_device(positions, thermal_noise):
    squares = lax.psum(jnp.sum(thermal_noise * thermal_noise, axis=(1, 2)), ("row", "col"))
    noise_length = jnp.sqrt(squares + 1e-06)
    basis_one = thermal_noise / noise_length[:, None, None]
    pos_cols, cols_one = (
        lax.all_gather(positions, "row", axis=1, tiled=True),
        lax.all_gather(basis_one, "row", axis=2, tiled=True),
    )
    pos_rows, rows_wide = (
        lax.all_gather(positions, "col", axis=1, tiled=True),
        lax.all_gather(basis_one, "col", axis=2, tiled=True),
    )
    image_one = half_image(
        pos_rows, pos_cols, rows_wide.astype(jnp.bfloat16), cols_one.astype(jnp.bfloat16), basis_one
    )
    alpha_one = lax.psum(jnp.sum(basis_one * image_one, axis=(1, 2)), ("row", "col"))
    remainder = image_one - alpha_one[:, None, None] * basis_one
    beta_squared = lax.psum(jnp.sum(remainder * remainder, axis=(1, 2)), ("row", "col"))
    beta_one = jnp.sqrt(beta_squared + 1e-06)
    basis_two = remainder / beta_one[:, None, None]
    narrow_two = basis_two.astype(jnp.bfloat16)
    cols_two = lax.all_gather(narrow_two, "row", axis=2, tiled=True)
    rows_two = lax.all_gather(narrow_two, "col", axis=2, tiled=True)
    image_two = half_image(pos_rows, pos_cols, rows_two, cols_two, basis_two)
    alpha_two = lax.psum(jnp.sum(basis_two * image_two, axis=(1, 2)), ("row", "col"))
    det_root = jnp.sqrt(alpha_one * alpha_two - beta_one * beta_one)
    trace_root = jnp.sqrt(alpha_one + alpha_two + 2.0 * det_root)
    weight_one = (alpha_one + det_root) / trace_root
    weight_two = beta_one / trace_root
    return (
        0.5
        * noise_length[:, None, None]
        * (weight_one[:, None, None] * basis_one + weight_two[:, None, None] * basis_two)
    )


def solution(mesh):
    specs = dict(
        mesh=mesh,
        in_specs=(P(None, ("row", "col")), P(None, None, ("row", "col"))),
        out_specs=P(None, None, ("row", "col")),
        check_vma=False,
    )

    def program(positions, thermal_noise):
        if fits(mesh, positions, thermal_noise):
            body = functools.partial(replicated, mesh)
        else:
            body = on_device
        return jax.shard_map(body, **specs)(positions, thermal_noise)

    return program
```

profile of v0, /device:TPU:0, one launch (start us, length us, event | category | flops | bytes accessed | tf_op | source)
XLA Modules:
  0.0 18.5 jit_solution(5761412265212178367)
XLA Ops:
  0.0 17.1 %lanczos.1 = f32[3,16,32]{2,1,0:T(8,128)} custom-call(f32[3,16,32]{2,1,0:T(8,128)} %bitcast.3, f32[3,16]{1,0:T(4,128)} %pos_ref.1), custom_call_target="tpu_custom_call" | custom-call | tf_op jit(solution)/shard_map/lanczos/pallas_call | solution.py:312
  17.1 1.3 %copy.4 = f32[32,3,16]{0,2,1:T(8,128)} copy(f32[32,3,16]{0,2,1:T(8,128)} %bitcast.2) | data formatting | bytes 12288
where the time goes:
time: 18.7 us; the launch traced here: 18.5 us
  Pallas kernels  17.1 us (91%)
  local copies, waits for them, and re-layouts  1.35 us (7%)
    pallas_call x1, Pallas kernels, replicated(): pl.pallas_call(functools.partial(replicated_kernel, rows, outer, inner),...  17.1 us
    unnamed x1, local copies, waits for them, and re-layouts  1.35 us

commit v1 on v0

v1 whole, which is shorter than its diff:
```python
import functools

import jax
import jax.numpy as jnp
from jax import lax
from jax.experimental import pallas as pl
from jax.experimental.pallas import tpu as pltpu
from jax.sharding import PartitionSpec as P

LANES = 128
LOGICAL = pl.DeviceIdType.LOGICAL
MUTUAL = 0
BLOCKS = ((0, 0), (1, 1), (2, 2), (0, 1), (0, 2), (1, 2))


def chip_bits(rows, cols):
    bits = [(1, 1)]
    weight = 2
    while weight < rows:
        bits.append((weight * cols, weight // 2))
        weight = 2 * weight
    weight = 2
    while weight < cols:
        bits.append((weight, weight // 2))
        weight = 2 * weight
    return bits


def replicated_kernel(
    rows,
    cols,
    noise_hbm,
    pos_hbm,
    out_ref,
    noise_ref,
    pos_ref,
    gathered,
    stage,
    own_ref,
    noise_full,
    pos_cols,
    pos_rows,
    mobility,
    narrow,
    image,
    load_sem,
    send_sem,
    recv_sem,
    grant,
):
    _, per_device, samples = noise_ref.shape
    particles = rows * cols * per_device
    f32, bf16 = jnp.float32, jnp.bfloat16
    my_row, my_col = lax.axis_index("row"), lax.axis_index("col")

    load_pos = pltpu.make_async_copy(pos_hbm, pos_ref, load_sem.at[0])
    load_noise = pltpu.make_async_copy(noise_hbm, noise_ref, load_sem.at[1])
    load_pos.start()
    load_noise.start()

    bits = chip_bits(rows, cols)
    chips = rows * cols // 2
    me = my_row * cols + my_col
    core = lax.rem(my_row, 2)
    mate = cols * (1 - 2 * core)
    my_code = 0
    device, ahead, level = {0: me}, {0: 0}, {0: 0}
    for index, (weight, height) in enumerate(bits):
        digit = lax.rem(me // weight, 2)
        my_code = my_code + (digit << index)
        sign = 1 - 2 * digit
        for code in range(1 << index):
            device[code + (1 << index)] = device[code] + weight * sign
            ahead[code + (1 << index)] = ahead[code] + height * sign
            level[code + (1 << index)] = level[code] + height
    order = sorted(range(chips), key=lambda code: (level[code], code))

    def both(code):
        return device[code], device[code] + mate

    barrier = pltpu.get_barrier_semaphore()
    pl.semaphore_signal(barrier, inc=1, device_id=me + mate, device_id_type=LOGICAL)
    greetings = 1
    for code in order[1:]:
        greetings = greetings + jnp.where(ahead[code] <= MUTUAL, 2, 0)

        @pl.when(ahead[code] >= -MUTUAL)
        def _(code=code):
            for target in both(code):
                pl.semaphore_signal(barrier, inc=1, device_id=target, device_id_type=LOGICAL)

    stage[...] = jnp.zeros_like(stage)
    own_ref[...] = jnp.zeros_like(own_ref)
    load_pos.wait()
    position = pos_ref[...]
    for term in range(3):
        piece = position.astype(bf16).astype(f32)
        stage[pl.ds(3 * term, 3), pl.ds(0, per_device)] = piece
        position = position - piece
    turned = jnp.transpose(stage[...])
    own_ref[:, pl.ds(3 * samples, 16)] = turned[0:per_device, :]

    pl.semaphore_wait(barrier, greetings)
    for code in order[:0:-1]:

        @pl.when(ahead[code] < -MUTUAL)
        def _(code=code):
            for target in both(code):
                pl.semaphore_signal(
                    grant.at[code], inc=1, device_id=target, device_id_type=LOGICAL
                )

    load_noise.wait()
    for b in range(3):
        own_ref[:, pl.ds(b * samples, samples)] = noise_ref[b]
    gathered[0, 0] = own_ref[...].astype(bf16)

    def send(code, side, target):
        pltpu.make_async_remote_copy(
            src_ref=gathered.at[0, 0],
            dst_ref=gathered.at[code, side],
            send_sem=send_sem.at[code],
            recv_sem=recv_sem.at[code],
            device_id=target,
            device_id_type=LOGICAL,
        ).start()

    def finished(ref, semaphore):
        pltpu.make_async_copy(ref, ref, semaphore).wait()

    @pl.when(my_code > 0)
    def _():
        for side in range(2):
            send(my_code, side, core * cols + side * mate)

    for code in order[:0:-1]:

        @pl.when((ahead[code] <= MUTUAL) & (my_code != code))
        def _(code=code):
            for side, target in enumerate(both(code)):
                send(code, side, target)

    send(0, 1, me + mate)

    def send_later(code):
        @pl.when(ahead[code] > MUTUAL)
        def _():
            pl.semaphore_wait(grant.at[code], 2)
            for side, target in enumerate(both(code)):
                send(code, side, target)

    lane = lax.broadcasted_iota(jnp.int32, (1, LANES), 1)
    field = lax.broadcasted_iota(jnp.int32, (LANES, 3 * LANES), 0) - 3 * samples
    target = lax.broadcasted_iota(jnp.int32, (LANES, 3 * LANES), 1) // LANES
    select = (field == target) | (field == target + 3) | (field == target + 6)
    over_lanes = select.astype(f32).astype(bf16)
    fields = 3 * samples
    field = lax.broadcasted_iota(jnp.int32, (fields + 3 * 16, LANES), 1)
    target = lax.broadcasted_iota(jnp.int32, (fields + 3 * 16, LANES), 0)
    coordinate = (target - fields) // 16
    moved = (field - fields == coordinate) | (field - fields == coordinate + 3)
    moved = moved | (field - fields == coordinate + 6)
    select = ((target < fields) & (field == target)) | ((target >= fields) & moved)
    turning = select.astype(f32).astype(bf16)
    tiles = particles // LANES

    def form(start, tile, on_diagonal):
        at_rows, at_lanes = pl.ds(start, 16), pl.ds(tile * LANES, LANES)
        d = [
            pos_cols[at_rows, pl.ds(a * LANES, LANES)] - pos_rows[pl.ds(a * 16, 16), at_lanes]
            for a in range(3)
        ]
        q = d[0] * d[0] + d[1] * d[1] + d[2] * d[2]
        if on_diagonal:
            row_label = start + lax.broadcasted_iota(jnp.int32, (16, LANES), 0)
            col_label = tile * LANES + lax.broadcasted_iota(jnp.int32, (16, LANES), 1)
            retain = row_label != col_label
            q = jnp.where(retain, q, 4.0)
        u = lax.rsqrt(q)
        r = q * u
        near = r < 2.0
        u2 = u * u
        f = jnp.where(near, 1.0 - 0.28125 * r, u * (0.75 + 0.5 * u2))
        if on_diagonal:
            f = jnp.where(retain, f, 0.0)
        h = u * jnp.where(near, 0.09375, u2 * (0.75 - 1.5 * u2))
        hd = [h * d[a] for a in range(3)]
        for n, (a, b) in enumerate(BLOCKS):
            element = hd[a] * d[b]
            if a == b:
                element = element + f
            mobility[n, at_rows, at_lanes] = element.astype(bf16)

    def rows_of(b):
        return pl.ds(b * samples, samples)

    def lanes_of(span):
        return pl.ds(span[0] * LANES, (span[1] - span[0]) * LANES)

    def fold(x):
        x = x[:samples] + x[samples : 2 * samples] + x[2 * samples :]
        parts = [x[:, start : start + LANES] for start in range(0, x.shape[1], LANES)]
        return functools.reduce(jnp.add, parts)

    def total(x):
        return jnp.sum(x, axis=1, keepdims=True)

    def thrice(x):
        return jnp.concatenate([x, x, x], axis=0)

    def product(pieces, rows_span, lanes_span):
        zero = jnp.zeros_like(pieces[0])
        columns = []
        for a, b in BLOCKS:
            column = [zero, zero, zero]
            column[a], column[b] = pieces[b], pieces[a]
            columns.append(jnp.concatenate(column, axis=0))
        left = jnp.concatenate(columns, axis=1)
        right = jnp.concatenate(
            [mobility[n, lanes_of(rows_span), lanes_of(lanes_span)] for n in range(6)], axis=0
        )
        return jnp.dot(left, right, preferred_element_type=f32)

    def noise_pieces(span):
        return [narrow[rows_of(b), lanes_of(span)] for b in range(3)]

    per_tile = LANES // (2 * per_device)
    half, last = tiles // 2, tiles - 1
    squares = jnp.zeros((samples, LANES), f32)
    own_turned = jnp.transpose(own_ref[...])

    def members(tile):
        return order[tile * per_tile : (tile + 1) * per_tile]

    def receive(tile):
        at = pl.ds(tile * LANES, LANES)
        for code in members(tile):
            if code:
                finished(gathered.at[code], recv_sem.at[code])
            else:
                finished(gathered.at[0, 1], recv_sem.at[0])
        packed = jnp.concatenate(
            [gathered[code].reshape(2 * per_device, LANES) for code in members(tile)], axis=0
        )
        pos_cols[at, :] = jnp.dot(packed, over_lanes, preferred_element_type=f32)
        turned = lax.dot_general(
            turning, packed, (((1,), (1,)), ((), ())), preferred_element_type=f32
        )
        pos_rows[:, at] = turned[fields:]
        noise_full[:, at] = turned[:fields]
        narrow[:, at] = turned[:fields].astype(bf16)
        if tile == 0:
            noise_full[:, pl.ds(0, per_device)] = own_turned[:fields]
        return fold(noise_full[:, at] * noise_full[:, at])

    for code in order[1:]:
        send_later(code)
    for tile in range(tiles):
        if tile == last:
            image[:, lanes_of((0, last))] = product(noise_pieces((0, last)), (0, last), (0, last))
        squares = squares + receive(tile)
        if tile == last:
            for step in range(LANES // 16):
                for other in range(last):
                    form(last * LANES + step * 16, other, False)
                form(last * LANES + step * 16, last, True)
            for step in range(LANES // 16):
                for other in range(last):
                    form(other * LANES + step * 16, last, False)
        else:

            @pl.loop(0, LANES // 16)
            def _(step, tile=tile):
                for other in range(tile + 1):
                    start = pl.multiple_of(tile * LANES + step * 16, 16)
                    form(start, other, other == tile)
                for other in range(tile):
                    start = pl.multiple_of(other * LANES + step * 16, 16)
                    form(start, tile, False)


    squares = total(squares)
    inverse = 1.0 / (squares + 1e-06)
    late = product(noise_pieces((last, tiles)), (last, tiles), (0, tiles))
    at_earlier, at_last = lanes_of((0, last)), lanes_of((last, tiles))
    at_late = product(noise_pieces((0, last)), (0, last), (last, tiles))
    first_image = jnp.concatenate(
        [image[:, at_earlier] + late[:, : last * LANES], at_late + late[:, last * LANES :]],
        axis=1,
    )

    coupled = total(fold(noise_full[...] * first_image))
    alpha_one = (squares + coupled) * inverse
    slope = (coupled - 1e-06) * inverse
    remainder = first_image - thrice(slope) * noise_full[...]
    remainders = fold(remainder * remainder)
    beta_squared = total(remainders) * inverse + 1e-06

    rounded = remainder.astype(bf16)
    cut = half * LANES
    low = [rounded[b * samples : (b + 1) * samples, :cut] for b in range(3)]
    high = [rounded[b * samples : (b + 1) * samples, cut:] for b in range(3)]
    twice = [piece + piece for piece in high]
    both_halves = [jnp.concatenate([x, y], axis=1) for x, y in zip(low, twice)]
    low_image = product(both_halves, (0, tiles), (0, half))
    high_image = product(high, (half, tiles), (half, tiles))
    quadratic = total(
        remainders
        + fold(remainder[:, :cut] * low_image)
        + fold(remainder[:, cut:] * high_image)
    )
    alpha_two = quadratic * inverse / beta_squared
    det_root = jnp.sqrt(alpha_one * alpha_two - beta_squared)
    trace_root = jnp.sqrt(alpha_one + alpha_two + 2.0 * det_root)
    scale = 0.5 / trace_root
    weight = (alpha_one + det_root) * scale
    result = thrice(weight) * noise_full[:, :LANES] + thrice(scale) * remainder[:, :LANES]
    result = jnp.transpose(result)[:per_device]
    for b in range(3):
        out_ref[b] = result[:, b * samples : (b + 1) * samples]

    finished(gathered.at[0, 1], send_sem.at[0])
    for code in range(1, chips):
        finished(gathered.at[code], send_sem.at[code])


def replicated(mesh, positions, thermal_noise):
    rows, cols = mesh.shape["row"], mesh.shape["col"]
    samples, _, per_device = thermal_noise.shape
    particles = rows * cols * per_device
    chips = rows * cols // 2
    f32, bf16 = jnp.float32, jnp.bfloat16
    vmem = pl.BlockSpec(memory_space=pltpu.VMEM)
    anywhere = pl.BlockSpec(memory_space=pl.ANY)
    out = pl.pallas_call(
        functools.partial(replicated_kernel, rows, cols),
        out_shape=jax.ShapeDtypeStruct((3, per_device, samples), f32),
        in_specs=[anywhere, anywhere],
        out_specs=vmem,
        scratch_shapes=[
            pltpu.VMEM((3, per_device, samples), f32),
            pltpu.VMEM((3, per_device), f32),
            pltpu.VMEM((chips, 2, per_device, LANES), bf16),
            pltpu.VMEM((16, LANES), f32),
            pltpu.VMEM((per_device, LANES), f32),
            pltpu.VMEM((3 * samples, particles), f32),
            pltpu.VMEM((particles, 3 * LANES), f32),
            pltpu.VMEM((3 * 16, particles), f32),
            pltpu.VMEM((6, particles, particles), bf16),
            pltpu.VMEM((3 * samples, particles), bf16),
            pltpu.VMEM((3 * samples, particles), f32),
            pltpu.SemaphoreType.DMA((2,)),
            pltpu.SemaphoreType.DMA((chips,)),
            pltpu.SemaphoreType.DMA((chips,)),
            pltpu.SemaphoreType.REGULAR((chips,)),
        ],
        compiler_params=pltpu.CompilerParams(collective_id=0, has_side_effects=True),
        name="lanczos",
    )(jnp.transpose(thermal_noise, (1, 2, 0)), positions)
    return jnp.transpose(out, (2, 0, 1))


def fits(mesh, positions, thermal_noise):
    rows, cols = mesh.shape["row"], mesh.shape["col"]
    samples, _, particles = thermal_noise.shape
    per_device = particles // (rows * cols)
    return (
        rows & (rows - 1) == 0
        and cols & (cols - 1) == 0
        and min(rows, cols) >= 2
        and 4 * samples == LANES
        and per_device == 16
        and particles % (2 * LANES) == 0
        and 12 * particles * particles <= 2**24
    )


def pair_tensor(rows_pos, cols_pos, retain):
    offsets = [rows_pos[a][None, :] - cols_pos[a][:, None] for a in range(3)]
    squared = offsets[0] * offsets[0] + offsets[1] * offsets[1] + offsets[2] * offsets[2]
    guarded = jnp.where(retain, squared, 4.0)
    inverse = lax.rsqrt(guarded)
    distance = guarded * inverse
    correlation = distance < 2.0
    inverse_cube = inverse * inverse * inverse
    inverse_fifth = inverse_cube * inverse * inverse
    isotropic = jnp.where(
        correlation, 1.0 - 0.28125 * distance, 0.75 * inverse + 0.5 * inverse_cube
    )
    dyadic = jnp.where(correlation, 0.09375 * inverse, 0.75 * inverse_cube - 1.5 * inverse_fifth)
    isotropic = jnp.where(retain, isotropic, 0.0)
    dyadic = jnp.where(retain, dyadic, 0.0)
    columns = []
    for b in range(3):
        elements = []
        for a in range(3):
            element = dyadic * offsets[a] * offsets[b]
            if a == b:
                element = element + isotropic
            elements.append(element)
        columns.append(jnp.stack(elements, axis=1))
    return jnp.stack(columns, axis=0)


def half_image(pos_rows, pos_cols, vec_rows, vec_cols, own_vector):
    row_devices = lax.axis_size("row")
    col_devices = lax.axis_size("col")
    row_index = lax.axis_index("row")
    col_index = lax.axis_index("col")
    samples = own_vector.shape[0]
    per_device = own_vector.shape[2]
    row_count = pos_rows.shape[1]
    row_label = row_index * col_devices * per_device + lax.iota(jnp.int32, row_count)
    group_size = min(row_devices, max(1, 128 // per_device))
    width = group_size * per_device
    group_count = row_devices // group_size
    sum_rows = jnp.zeros((samples, 3, row_count), jnp.float32)
    sum_cols = jnp.zeros((samples, 3, per_device * row_devices), jnp.float32)

    def add_group(group, totals):
        sum_rows, sum_cols = totals
        start = group * width
        cols_pos = lax.dynamic_slice_in_dim(pos_cols, start, width, 1)
        cols_vec = lax.dynamic_slice_in_dim(vec_cols, start, width, 2)
        local_cols = lax.iota(jnp.int32, width)
        segment = group * group_size + local_cols // per_device
        col_label = (segment * col_devices + col_index) * per_device + local_cols % per_device
        keep = segment >= row_index
        upper = (segment != row_index)[:, None] | (row_label[None, :] < col_label[:, None])
        retain = keep[:, None] & upper & (row_label[None, :] != col_label[:, None])
        tensor = pair_tensor(pos_rows, cols_pos, retain).astype(jnp.bfloat16)
        sum_rows = sum_rows + jnp.einsum(
            "kbj,bjai->kai", cols_vec, tensor, preferred_element_type=jnp.float32
        )
        credit = jnp.einsum("kai,bjai->kbj", vec_rows, tensor, preferred_element_type=jnp.float32)
        previous = lax.dynamic_slice_in_dim(sum_cols, start, width, 2)
        sum_cols = lax.dynamic_update_slice_in_dim(sum_cols, previous + credit, start, 2)
        return (sum_rows, sum_cols)

    totals = (sum_rows, sum_cols)
    totals = lax.fori_loop(row_index // group_size, group_count, add_group, totals)
    sum_rows, sum_cols = totals
    mobility_image = own_vector + lax.psum_scatter(sum_rows, "col", scatter_dimension=2, tiled=True)
    return mobility_image + lax.psum_scatter(sum_cols, "row", scatter_dimension=2, tiled=True)


def on_device(positions, thermal_noise):
    squares = lax.psum(jnp.sum(thermal_noise * thermal_noise, axis=(1, 2)), ("row", "col"))
    noise_length = jnp.sqrt(squares + 1e-06)
    basis_one = thermal_noise / noise_length[:, None, None]
    pos_cols, cols_one = (
        lax.all_gather(positions, "row", axis=1, tiled=True),
        lax.all_gather(basis_one, "row", axis=2, tiled=True),
    )
    pos_rows, rows_wide = (
        lax.all_gather(positions, "col", axis=1, tiled=True),
        lax.all_gather(basis_one, "col", axis=2, tiled=True),
    )
    image_one = half_image(
        pos_rows, pos_cols, rows_wide.astype(jnp.bfloat16), cols_one.astype(jnp.bfloat16), basis_one
    )
    alpha_one = lax.psum(jnp.sum(basis_one * image_one, axis=(1, 2)), ("row", "col"))
    remainder = image_one - alpha_one[:, None, None] * basis_one
    beta_squared = lax.psum(jnp.sum(remainder * remainder, axis=(1, 2)), ("row", "col"))
    beta_one = jnp.sqrt(beta_squared + 1e-06)
    basis_two = remainder / beta_one[:, None, None]
    narrow_two = basis_two.astype(jnp.bfloat16)
    cols_two = lax.all_gather(narrow_two, "row", axis=2, tiled=True)
    rows_two = lax.all_gather(narrow_two, "col", axis=2, tiled=True)
    image_two = half_image(pos_rows, pos_cols, rows_two, cols_two, basis_two)
    alpha_two = lax.psum(jnp.sum(basis_two * image_two, axis=(1, 2)), ("row", "col"))
    det_root = jnp.sqrt(alpha_one * alpha_two - beta_one * beta_one)
    trace_root = jnp.sqrt(alpha_one + alpha_two + 2.0 * det_root)
    weight_one = (alpha_one + det_root) / trace_root
    weight_two = beta_one / trace_root
    return (
        0.5
        * noise_length[:, None, None]
        * (weight_one[:, None, None] * basis_one + weight_two[:, None, None] * basis_two)
    )


def solution(mesh):
    specs = dict(
        mesh=mesh,
        in_specs=(P(None, ("row", "col")), P(None, None, ("row", "col"))),
        out_specs=P(None, None, ("row", "col")),
        check_vma=False,
    )

    def program(positions, thermal_noise):
        if fits(mesh, positions, thermal_noise):
            body = functools.partial(replicated, mesh)
        else:
            body = on_device
        return jax.shard_map(body, **specs)(positions, thermal_noise)

    return program
```

time: 18.7 us -> 15.6 us (0.83)
  Pallas kernels: 17.1 us -> 14 us
    pallas_call x1, Pallas kernels: 17.1 us -> 14 us  [replicated(): pl.pallas_call(functools.partial(replicated_kernel, rows, cols), out_shap...]
where the time goes in v1:
time: 15.6 us; the launch traced here: 15.3 us
  Pallas kernels  14 us (90%)
  local copies, waits for them, and re-layouts  1.35 us (9%)
    pallas_call x1, Pallas kernels, replicated(): pl.pallas_call(functools.partial(replicated_kernel, rows, cols), out_shap...  14 us
    unnamed x1, local copies, waits for them, and re-layouts  1.35 us

profile of v1, /device:TPU:0, one launch (start us, length us, event | category | flops | bytes accessed | tf_op | source)
XLA Modules:
  0.0 15.3 jit_solution(14860335712059640189)
XLA Ops:
  0.0 14.0 %lanczos.1 = f32[3,16,32]{2,1,0:T(8,128)} custom-call(f32[3,16,32]{2,1,0:T(8,128)} %bitcast.3, f32[3,16]{1,0:T(4,128)} %pos_hbm.1), custom_call_target="tpu_custom_call" | custom-call | tf_op jit(solution)/shard_map/lanczos/pallas_call | solution.py:335
  14.0 1.3 %copy.4 = f32[32,3,16]{0,2,1:T(8,128)} copy(f32[32,3,16]{0,2,1:T(8,128)} %bitcast.2) | data formatting | bytes 12288

commit v2 on v1

--- a/solution.py
+++ b/solution.py
@@ -334,7 +334,7 @@
     anywhere = pl.BlockSpec(memory_space=pl.ANY)
     out = pl.pallas_call(
         functools.partial(replicated_kernel, rows, cols),
-        out_shape=jax.ShapeDtypeStruct((3, per_device, samples), f32),
+        out_shape=pltpu.VMEM((3, per_device, samples), f32),
         in_specs=[anywhere, anywhere],
         out_specs=vmem,
         scratch_shapes=[

time: 15.6 us -> 14.2 us (0.910)
  local copies, waits for them, and re-layouts: 1.35 us -> 0.61 us
  Pallas kernels: 14 us -> 13.4 us
    unnamed x1, local copies, waits for them, and re-layouts: 1.35 us -> 0.61 us
    pallas_call x1, Pallas kernels: 14 us -> 13.4 us  [replicated(): pl.pallas_call(functools.partial(replicated_kernel, rows, cols), out_shap...]
where the time goes in v2:
time: 14.2 us; the launch traced here: 14 us
  Pallas kernels  13.4 us (94%)
  local copies, waits for them, and re-layouts  0.61 us (4%)
    pallas_call x1, Pallas kernels, replicated(): pl.pallas_call(functools.partial(replicated_kernel, rows, cols), out_shap...  13.4 us
    unnamed x1, local copies, waits for them, and re-layouts  0.61 us

profile of v2, /device:TPU:0, one launch (start us, length us, event | category | flops | bytes accessed | tf_op | source)
XLA Modules:
  0.0 14.0 jit_solution(16319008139180203421)
XLA Ops:
  0.0 13.4 %lanczos.1 = f32[3,16,32]{2,1,0:T(8,128)S(1)} custom-call(f32[3,16,32]{2,1,0:T(8,128)} %bitcast.3, f32[3,16]{1,0:T(4,128)} %pos_hbm.1), custom_call_target="tpu_custom_call" | custom-call | tf_op jit(solution)/shard_map/lanczos/pallas_call | solution.py:335
  13.4 0.6 %copy.4 = f32[32,3,16]{0,2,1:T(8,128)} copy(f32[32,3,16]{0,2,1:T(8,128)S(1)} %bitcast.2) | data formatting | bytes 12288

commit v3 on v2

--- a/solution.py
+++ b/solution.py
@@ -189,7 +189,7 @@
             element = hd[a] * d[b]
             if a == b:
                 element = element + f
-            mobility[n, at_rows, at_lanes] = element.astype(bf16)
+            mobility[n, tile, at_rows, :] = element.astype(bf16)
 
     def rows_of(b):
         return pl.ds(b * samples, samples)
@@ -208,25 +208,30 @@
     def thrice(x):
         return jnp.concatenate([x, x, x], axis=0)
 
-    def product(pieces, rows_span, lanes_span):
+    def spread(pieces):
         zero = jnp.zeros_like(pieces[0])
         columns = []
         for a, b in BLOCKS:
             column = [zero, zero, zero]
             column[a], column[b] = pieces[b], pieces[a]
             columns.append(jnp.concatenate(column, axis=0))
-        left = jnp.concatenate(columns, axis=1)
-        right = jnp.concatenate(
-            [mobility[n, lanes_of(rows_span), lanes_of(lanes_span)] for n in range(6)], axis=0
+        return jnp.concatenate(columns, axis=1)
+
+    def onto(pieces, span, tile):
+        right = jnp.concatenate([mobility[n, tile, lanes_of(span), :] for n in range(6)], axis=0)
+        return jnp.dot(spread(pieces), right, preferred_element_type=f32)
+
+    def back(pieces, other, tile):
+        at = lanes_of((other, other + 1))
+        right = jnp.concatenate([mobility[n, tile, at, :] for n in range(6)], axis=1)
+        return lax.dot_general(
+            spread(pieces), right, (((1,), (1,)), ((), ())), preferred_element_type=f32
         )
-        return jnp.dot(left, right, preferred_element_type=f32)
 
     def noise_pieces(span):
         return [narrow[rows_of(b), lanes_of(span)] for b in range(3)]
 
     per_tile = LANES // (2 * per_device)
-    half, last = tiles // 2, tiles - 1
-    squares = jnp.zeros((samples, LANES), f32)
     own_turned = jnp.transpose(own_ref[...])
 
     def members(tile):
@@ -251,44 +256,25 @@
         narrow[:, at] = turned[:fields].astype(bf16)
         if tile == 0:
             noise_full[:, pl.ds(0, per_device)] = own_turned[:fields]
-        return fold(noise_full[:, at] * noise_full[:, at])
 
     for code in order[1:]:
         send_later(code)
     for tile in range(tiles):
-        if tile == last:
-            image[:, lanes_of((0, last))] = product(noise_pieces((0, last)), (0, last), (0, last))
-        squares = squares + receive(tile)
-        if tile == last:
+        receive(tile)
+        gained = None
+        for other in range(tile + 1):
             for step in range(LANES // 16):
-                for other in range(last):
-                    form(last * LANES + step * 16, other, False)
-                form(last * LANES + step * 16, last, True)
-            for step in range(LANES // 16):
-                for other in range(last):
-                    form(other * LANES + step * 16, last, False)
-        else:
-
-            @pl.loop(0, LANES // 16)
-            def _(step, tile=tile):
-                for other in range(tile + 1):
-                    start = pl.multiple_of(tile * LANES + step * 16, 16)
-                    form(start, other, other == tile)
-                for other in range(tile):
-                    start = pl.multiple_of(other * LANES + step * 16, 16)
-                    form(start, tile, False)
-
-
-    squares = total(squares)
+                form(other * LANES + step * 16, tile, other == tile)
+            part = onto(noise_pieces((other, other + 1)), (other, other + 1), tile)
+            gained = part if gained is None else gained + part
+            if other < tile:
+                at = lanes_of((other, other + 1))
+                image[:, at] = image[:, at] + back(noise_pieces((tile, tile + 1)), other, tile)
+        image[:, lanes_of((tile, tile + 1))] = gained
+
+    squares = total(fold(noise_full[...] * noise_full[...]))
     inverse = 1.0 / (squares + 1e-06)
-    late = product(noise_pieces((last, tiles)), (last, tiles), (0, tiles))
-    at_earlier, at_last = lanes_of((0, last)), lanes_of((last, tiles))
-    at_late = product(noise_pieces((0, last)), (0, last), (last, tiles))
-    first_image = jnp.concatenate(
-        [image[:, at_earlier] + late[:, : last * LANES], at_late + late[:, last * LANES :]],
-        axis=1,
-    )
-
+    first_image = image[...]
     coupled = total(fold(noise_full[...] * first_image))
     alpha_one = (squares + coupled) * inverse
     slope = (coupled - 1e-06) * inverse
@@ -297,18 +283,19 @@
     beta_squared = total(remainders) * inverse + 1e-06
 
     rounded = remainder.astype(bf16)
-    cut = half * LANES
-    low = [rounded[b * samples : (b + 1) * samples, :cut] for b in range(3)]
-    high = [rounded[b * samples : (b + 1) * samples, cut:] for b in range(3)]
-    twice = [piece + piece for piece in high]
-    both_halves = [jnp.concatenate([x, y], axis=1) for x, y in zip(low, twice)]
-    low_image = product(both_halves, (0, tiles), (0, half))
-    high_image = product(high, (half, tiles), (half, tiles))
-    quadratic = total(
-        remainders
-        + fold(remainder[:, :cut] * low_image)
-        + fold(remainder[:, cut:] * high_image)
-    )
+    twice = rounded + rounded
+    parts = remainders
+    for tile in range(tiles):
+        at = slice(tile * LANES, (tile + 1) * LANES)
+        pieces = []
+        for b in range(3):
+            rows_at = slice(b * samples, (b + 1) * samples)
+            piece = rounded[rows_at, at]
+            if tile:
+                piece = jnp.concatenate([twice[rows_at, : tile * LANES], piece], axis=1)
+            pieces.append(piece)
+        parts = parts + fold(remainder[:, at] * onto(pieces, (0, tile + 1), tile))
+    quadratic = total(parts)
     alpha_two = quadratic * inverse / beta_squared
     det_root = jnp.sqrt(alpha_one * alpha_two - beta_squared)
     trace_root = jnp.sqrt(alpha_one + alpha_two + 2.0 * det_root)
@@ -346,7 +333,7 @@
             pltpu.VMEM((3 * samples, particles), f32),
             pltpu.VMEM((particles, 3 * LANES), f32),
             pltpu.VMEM((3 * 16, particles), f32),
-            pltpu.VMEM((6, particles, particles), bf16),
+            pltpu.VMEM((6, particles // LANES, particles, LANES), bf16),
             pltpu.VMEM((3 * samples, particles), bf16),
             pltpu.VMEM((3 * samples, particles), f32),
             pltpu.SemaphoreType.DMA((2,)),

time: 14.2 us -> 13.2 us (0.930)
  Pallas kernels: 13.4 us -> 12.4 us
    pallas_call x1, Pallas kernels: 13.4 us -> 12.4 us  [replicated(): pl.pallas_call(functools.partial(replicated_kernel, rows, cols), out_shap...]
where the time goes in v3:
time: 13.2 us; the launch traced here: 13 us
  Pallas kernels  12.4 us (94%)
  local copies, waits for them, and re-layouts  0.61 us (5%)
    pallas_call x1, Pallas kernels, replicated(): pl.pallas_call(functools.partial(replicated_kernel, rows, cols), out_shap...  12.4 us
    unnamed x1, local copies, waits for them, and re-layouts  0.61 us

profile of v3, /device:TPU:0, one launch (start us, length us, event | category | flops | bytes accessed | tf_op | source)
XLA Modules:
  0.0 13.0 jit_solution(9050771232538980217)
XLA Ops:
  0.0 12.4 %lanczos.1 = f32[3,16,32]{2,1,0:T(8,128)S(1)} custom-call(f32[3,16,32]{2,1,0:T(8,128)} %bitcast.3, f32[3,16]{1,0:T(4,128)} %pos_hbm.1), custom_call_target="tpu_custom_call" | custom-call | tf_op jit(solution)/shard_map/lanczos/pallas_call | solution.py:322
  12.4 0.6 %copy.4 = f32[32,3,16]{0,2,1:T(8,128)} copy(f32[32,3,16]{0,2,1:T(8,128)S(1)} %bitcast.2) | data formatting | bytes 12288

commit v4 on v3

--- a/solution.py
+++ b/solution.py
@@ -74,6 +74,11 @@
             ahead[code + (1 << index)] = ahead[code] + height * sign
             level[code + (1 << index)] = level[code] + height
     order = sorted(range(chips), key=lambda code: (level[code], code))
+    place = {code: index for index, code in enumerate(order)}
+    my_place = 0
+    for code in order[1:]:
+        my_place = my_place + jnp.where(my_code == code, place[code], 0)
+    per_tile = LANES // (2 * per_device)
 
     def both(code):
         return device[code], device[code] + mate
@@ -100,7 +105,31 @@
     turned = jnp.transpose(stage[...])
     own_ref[:, pl.ds(3 * samples, 16)] = turned[0:per_device, :]
 
+    load_noise.wait()
+    for b in range(3):
+        own_ref[:, pl.ds(b * samples, samples)] = noise_ref[b]
+    gathered[0] = own_ref[...].astype(bf16)
+
     pl.semaphore_wait(barrier, greetings)
+
+    def send(spot, side, target):
+        pltpu.make_async_remote_copy(
+            src_ref=gathered.at[0],
+            dst_ref=gathered.at[2 * spot + side],
+            send_sem=send_sem.at[0],
+            recv_sem=recv_sem.at[spot // per_tile],
+            device_id=target,
+            device_id_type=LOGICAL,
+        ).start()
+
+    def finished(ref, semaphore):
+        pltpu.make_async_copy(ref, ref, semaphore).wait()
+
+    @pl.when(my_code > 0)
+    def _():
+        for side in range(2):
+            send(my_place, side, core * cols + side * mate)
+
     for code in order[:0:-1]:
 
         @pl.when(ahead[code] < -MUTUAL)
@@ -110,35 +139,12 @@
                     grant.at[code], inc=1, device_id=target, device_id_type=LOGICAL
                 )
 
-    load_noise.wait()
-    for b in range(3):
-        own_ref[:, pl.ds(b * samples, samples)] = noise_ref[b]
-    gathered[0, 0] = own_ref[...].astype(bf16)
-
-    def send(code, side, target):
-        pltpu.make_async_remote_copy(
-            src_ref=gathered.at[0, 0],
-            dst_ref=gathered.at[code, side],
-            send_sem=send_sem.at[code],
-            recv_sem=recv_sem.at[code],
-            device_id=target,
-            device_id_type=LOGICAL,
-        ).start()
-
-    def finished(ref, semaphore):
-        pltpu.make_async_copy(ref, ref, semaphore).wait()
-
-    @pl.when(my_code > 0)
-    def _():
-        for side in range(2):
-            send(my_code, side, core * cols + side * mate)
-
     for code in order[:0:-1]:
 
         @pl.when((ahead[code] <= MUTUAL) & (my_code != code))
         def _(code=code):
             for side, target in enumerate(both(code)):
-                send(code, side, target)
+                send(place[code], side, target)
 
     send(0, 1, me + mate)
 
@@ -147,7 +153,7 @@
         def _():
             pl.semaphore_wait(grant.at[code], 2)
             for side, target in enumerate(both(code)):
-                send(code, side, target)
+                send(place[code], side, target)
 
     lane = lax.broadcasted_iota(jnp.int32, (1, LANES), 1)
     field = lax.broadcasted_iota(jnp.int32, (LANES, 3 * LANES), 0) - 3 * samples
@@ -205,6 +211,9 @@
     def total(x):
         return jnp.sum(x, axis=1, keepdims=True)
 
+    def total_row(x):
+        return jnp.sum(jnp.transpose(x), axis=0, keepdims=True)
+
     def thrice(x):
         return jnp.concatenate([x, x, x], axis=0)
 
@@ -217,7 +226,7 @@
             columns.append(jnp.concatenate(column, axis=0))
         return jnp.concatenate(columns, axis=1)
 
-    def onto(pieces, span, tile):
+    def onto_wide(pieces, span, tile):
         right = jnp.concatenate([mobility[n, tile, lanes_of(span), :] for n in range(6)], axis=0)
         return jnp.dot(spread(pieces), right, preferred_element_type=f32)
 
@@ -228,10 +237,28 @@
             spread(pieces), right, (((1,), (1,)), ((), ())), preferred_element_type=f32
         )
 
+    def blockwise(pieces, dot):
+        sums = [None] * 3
+        for n, (a, b) in enumerate(BLOCKS):
+            if a == b:
+                parts = [(a, dot(pieces[a], n))]
+            else:
+                part = dot(jnp.concatenate([pieces[b], pieces[a]], axis=0), n)
+                parts = [(a, part[:samples]), (b, part[samples:])]
+            for c, part in parts:
+                sums[c] = part if sums[c] is None else sums[c] + part
+        return jnp.concatenate(sums, axis=0)
+
+    def onto(pieces, span, tile):
+        def dot(left, n):
+            right = mobility[n, tile, lanes_of(span), :]
+            return jnp.dot(left, right, preferred_element_type=f32)
+
+        return blockwise(pieces, dot)
+
     def noise_pieces(span):
         return [narrow[rows_of(b), lanes_of(span)] for b in range(3)]
 
-    per_tile = LANES // (2 * per_device)
     own_turned = jnp.transpose(own_ref[...])
 
     def members(tile):
@@ -239,14 +266,10 @@
 
     def receive(tile):
         at = pl.ds(tile * LANES, LANES)
-        for code in members(tile):
-            if code:
-                finished(gathered.at[code], recv_sem.at[code])
-            else:
-                finished(gathered.at[0, 1], recv_sem.at[0])
-        packed = jnp.concatenate(
-            [gathered[code].reshape(2 * per_device, LANES) for code in members(tile)], axis=0
-        )
+        blocks = 2 * per_tile
+        first = max(tile * blocks, 1)
+        finished(gathered.at[pl.ds(first, (tile + 1) * blocks - first)], recv_sem.at[tile])
+        packed = gathered[pl.ds(tile * blocks, blocks)].reshape(LANES, LANES)
         pos_cols[at, :] = jnp.dot(packed, over_lanes, preferred_element_type=f32)
         turned = lax.dot_general(
             turning, packed, (((1,), (1,)), ((), ())), preferred_element_type=f32
@@ -265,22 +288,20 @@
         for other in range(tile + 1):
             for step in range(LANES // 16):
                 form(other * LANES + step * 16, tile, other == tile)
-            part = onto(noise_pieces((other, other + 1)), (other, other + 1), tile)
+            part = onto_wide(noise_pieces((other, other + 1)), (other, other + 1), tile)
             gained = part if gained is None else gained + part
             if other < tile:
                 at = lanes_of((other, other + 1))
                 image[:, at] = image[:, at] + back(noise_pieces((tile, tile + 1)), other, tile)
         image[:, lanes_of((tile, tile + 1))] = gained
 
-    squares = total(fold(noise_full[...] * noise_full[...]))
-    inverse = 1.0 / (squares + 1e-06)
+    square_parts = fold(noise_full[...] * noise_full[...])
+    inverse = 1.0 / (total(square_parts) + 1e-06)
     first_image = image[...]
-    coupled = total(fold(noise_full[...] * first_image))
-    alpha_one = (squares + coupled) * inverse
-    slope = (coupled - 1e-06) * inverse
+    coupled_parts = fold(noise_full[...] * first_image)
+    slope = (total(coupled_parts) - 1e-06) * inverse
     remainder = first_image - thrice(slope) * noise_full[...]
     remainders = fold(remainder * remainder)
-    beta_squared = total(remainders) * inverse + 1e-06
 
     rounded = remainder.astype(bf16)
     twice = rounded + rounded
@@ -295,20 +316,23 @@
                 piece = jnp.concatenate([twice[rows_at, : tile * LANES], piece], axis=1)
             pieces.append(piece)
         parts = parts + fold(remainder[:, at] * onto(pieces, (0, tile + 1), tile))
-    quadratic = total(parts)
-    alpha_two = quadratic * inverse / beta_squared
+
+    squares, coupled = total_row(square_parts), total_row(coupled_parts)
+    inverse = 1.0 / (squares + 1e-06)
+    alpha_one = (squares + coupled) * inverse
+    beta_squared = total_row(remainders) * inverse + 1e-06
+    ratio = inverse / beta_squared
+    own_remainder = jnp.transpose(remainder[:, :LANES])[:per_device]
+    alpha_two = total_row(parts) * ratio
     det_root = jnp.sqrt(alpha_one * alpha_two - beta_squared)
     trace_root = jnp.sqrt(alpha_one + alpha_two + 2.0 * det_root)
     scale = 0.5 / trace_root
     weight = (alpha_one + det_root) * scale
-    result = thrice(weight) * noise_full[:, :LANES] + thrice(scale) * remainder[:, :LANES]
-    result = jnp.transpose(result)[:per_device]
     for b in range(3):
-        out_ref[b] = result[:, b * samples : (b + 1) * samples]
-
-    finished(gathered.at[0, 1], send_sem.at[0])
-    for code in range(1, chips):
-        finished(gathered.at[code], send_sem.at[code])
+        own = own_remainder[:, b * samples : (b + 1) * samples]
+        out_ref[b] = weight * noise_ref[b] + scale * own
+
+    finished(gathered.at[pl.ds(1, 2 * chips - 1)], send_sem.at[0])
 
 
 def replicated(mesh, positions, thermal_noise):
@@ -327,7 +351,7 @@
         scratch_shapes=[
             pltpu.VMEM((3, per_device, samples), f32),
             pltpu.VMEM((3, per_device), f32),
-            pltpu.VMEM((chips, 2, per_device, LANES), bf16),
+            pltpu.VMEM((2 * chips, per_device, LANES), bf16),
             pltpu.VMEM((16, LANES), f32),
             pltpu.VMEM((per_device, LANES), f32),
             pltpu.VMEM((3 * samples, particles), f32),
@@ -337,8 +361,8 @@
             pltpu.VMEM((3 * samples, particles), bf16),
             pltpu.VMEM((3 * samples, particles), f32),
             pltpu.SemaphoreType.DMA((2,)),
-            pltpu.SemaphoreType.DMA((chips,)),
-            pltpu.SemaphoreType.DMA((chips,)),
+            pltpu.SemaphoreType.DMA((1,)),
+            pltpu.SemaphoreType.DMA((particles // LANES,)),
             pltpu.SemaphoreType.REGULAR((chips,)),
         ],
         compiler_params=pltpu.CompilerParams(collective_id=0, has_side_effects=True),

time: 13.2 us -> 12.7 us (0.962)
  Pallas kernels: 12.4 us -> 11.8 us
    pallas_call x1, Pallas kernels: 12.4 us -> 11.8 us  [replicated(): pl.pallas_call(functools.partial(replicated_kernel, rows, cols), out_shap...]
where the time goes in v4:
time: 12.7 us; the launch traced here: 12.4 us
  Pallas kernels  11.8 us (93%)
  local copies, waits for them, and re-layouts  0.61 us (5%)
    pallas_call x1, Pallas kernels, replicated(): pl.pallas_call(functools.partial(replicated_kernel, rows, cols), out_shap...  11.8 us
    unnamed x1, local copies, waits for them, and re-layouts  0.61 us

profile of v4, /device:TPU:0, one launch (start us, length us, event | category | flops | bytes accessed | tf_op | source)
XLA Modules:
  0.0 12.4 jit_solution(12674689674699159955)
XLA Ops:
  0.0 11.8 %lanczos.1 = f32[3,16,32]{2,1,0:T(8,128)S(1)} custom-call(f32[3,16,32]{2,1,0:T(8,128)} %bitcast.3, f32[3,16]{1,0:T(4,128)} %pos_hbm.1), custom_call_target="tpu_custom_call" | custom-call | tf_op jit(solution)/shard_map/lanczos/pallas_call | solution.py:346
  11.8 0.6 %copy.4 = f32[32,3,16]{0,2,1:T(8,128)} copy(f32[32,3,16]{0,2,1:T(8,128)S(1)} %bitcast.2) | data formatting | bytes 12288

commit v5 on v4

--- a/solution.py
+++ b/solution.py
@@ -66,6 +66,8 @@
     my_code = 0
     device, ahead, level = {0: me}, {0: 0}, {0: 0}
     for index, (weight, height) in enumerate(bits):
+        scale = 600 if 2 <= weight < cols else 600
+        height = height * scale + (1 << index)
         digit = lax.rem(me // weight, 2)
         my_code = my_code + (digit << index)
         sign = 1 - 2 * digit
@@ -95,7 +97,6 @@
                 pl.semaphore_signal(barrier, inc=1, device_id=target, device_id_type=LOGICAL)
 
     stage[...] = jnp.zeros_like(stage)
-    own_ref[...] = jnp.zeros_like(own_ref)
     load_pos.wait()
     position = pos_ref[...]
     for term in range(3):
@@ -103,12 +104,13 @@
         stage[pl.ds(3 * term, 3), pl.ds(0, per_device)] = piece
         position = position - piece
     turned = jnp.transpose(stage[...])
-    own_ref[:, pl.ds(3 * samples, 16)] = turned[0:per_device, :]
 
     load_noise.wait()
-    for b in range(3):
-        own_ref[:, pl.ds(b * samples, samples)] = noise_ref[b]
-    gathered[0] = own_ref[...].astype(bf16)
+    tail = jnp.zeros((per_device, LANES - 3 * samples - 16), f32)
+    own = [noise_ref[b] for b in range(3)] + [turned[0:per_device, :], tail]
+    own = jnp.concatenate(own, axis=1)
+    gathered[0] = own.astype(bf16)
+    own_ref[...] = own
 
     pl.semaphore_wait(barrier, greetings)
 
@@ -127,8 +129,8 @@
 
     @pl.when(my_code > 0)
     def _():
-        for side in range(2):
-            send(my_place, side, core * cols + side * mate)
+        send(my_place, core, 0)
+        send(my_place, 1 - core, cols)
 
     for code in order[:0:-1]:
 

time: 12.7 us -> 12.4 us (0.976)
  Pallas kernels: 11.8 us -> 11.6 us
    pallas_call x1, Pallas kernels: 11.8 us -> 11.6 us  [replicated(): pl.pallas_call(functools.partial(replicated_kernel, rows, cols), out_shap...]
where the time goes in v5:
time: 12.4 us; the launch traced here: 12.2 us
  Pallas kernels  11.6 us (94%)
  local copies, waits for them, and re-layouts  0.61 us (5%)
    pallas_call x1, Pallas kernels, replicated(): pl.pallas_call(functools.partial(replicated_kernel, rows, cols), out_shap...  11.6 us
    unnamed x1, local copies, waits for them, and re-layouts  0.61 us

profile of v5, /device:TPU:0, one launch (start us, length us, event | category | flops | bytes accessed | tf_op | source)
XLA Modules:
  0.0 12.2 jit_solution(9500298218936469715)
XLA Ops:
  0.0 11.6 %lanczos.1 = f32[3,16,32]{2,1,0:T(8,128)S(1)} custom-call(f32[3,16,32]{2,1,0:T(8,128)} %bitcast.3, f32[3,16]{1,0:T(4,128)} %pos_hbm.1), custom_call_target="tpu_custom_call" | custom-call | tf_op jit(solution)/shard_map/lanczos/pallas_call | solution.py:348
  11.6 0.6 %copy.4 = f32[32,3,16]{0,2,1:T(8,128)} copy(f32[32,3,16]{0,2,1:T(8,128)S(1)} %bitcast.2) | data formatting | bytes 12288

commit v6 on v5

--- a/solution.py
+++ b/solution.py
@@ -9,7 +9,6 @@
 
 LANES = 128
 LOGICAL = pl.DeviceIdType.LOGICAL
-MUTUAL = 0
 BLOCKS = ((0, 0), (1, 1), (2, 2), (0, 1), (0, 2), (1, 2))
 
 
@@ -66,8 +65,8 @@
     my_code = 0
     device, ahead, level = {0: me}, {0: 0}, {0: 0}
     for index, (weight, height) in enumerate(bits):
-        scale = 600 if 2 <= weight < cols else 600
-        height = height * scale + (1 << index)
+        step = 18 if 2 <= weight < cols else 20
+        height = height * step * chips + (1 << index)
         digit = lax.rem(me // weight, 2)
         my_code = my_code + (digit << index)
         sign = 1 - 2 * digit
@@ -89,9 +88,9 @@
     pl.semaphore_signal(barrier, inc=1, device_id=me + mate, device_id_type=LOGICAL)
     greetings = 1
     for code in order[1:]:
-        greetings = greetings + jnp.where(ahead[code] <= MUTUAL, 2, 0)
-
-        @pl.when(ahead[code] >= -MUTUAL)
+        greetings = greetings + jnp.where(ahead[code] < 0, 2, 0)
+
+        @pl.when(ahead[code] > 0)
         def _(code=code):
             for target in both(code):
                 pl.semaphore_signal(barrier, inc=1, device_id=target, device_id_type=LOGICAL)
@@ -134,7 +133,7 @@
 
     for code in order[:0:-1]:
 
-        @pl.when(ahead[code] < -MUTUAL)
+        @pl.when(ahead[code] < 0)
         def _(code=code):
             for target in both(code):
                 pl.semaphore_signal(
@@ -143,7 +142,7 @@
 
     for code in order[:0:-1]:
 
-        @pl.when((ahead[code] <= MUTUAL) & (my_code != code))
+        @pl.when((ahead[code] < 0) & (my_code != code))
         def _(code=code):
             for side, target in enumerate(both(code)):
                 send(place[code], side, target)
@@ -151,7 +150,7 @@
     send(0, 1, me + mate)
 
     def send_later(code):
-        @pl.when(ahead[code] > MUTUAL)
+        @pl.when(ahead[code] > 0)
         def _():
             pl.semaphore_wait(grant.at[code], 2)
             for side, target in enumerate(both(code)):
@@ -284,18 +283,31 @@
 
     for code in order[1:]:
         send_later(code)
-    for tile in range(tiles):
-        receive(tile)
-        gained = None
-        for other in range(tile + 1):
-            for step in range(LANES // 16):
-                form(other * LANES + step * 16, tile, other == tile)
+    def spread_products(tile, others, gained=None):
+        for other in others:
             part = onto_wide(noise_pieces((other, other + 1)), (other, other + 1), tile)
             gained = part if gained is None else gained + part
             if other < tile:
                 at = lanes_of((other, other + 1))
                 image[:, at] = image[:, at] + back(noise_pieces((tile, tile + 1)), other, tile)
-        image[:, lanes_of((tile, tile + 1))] = gained
+        return gained
+
+    held = []
+    for tile in range(tiles):
+        receive(tile)
+        for late in held:
+            image[:, lanes_of((late, late + 1))] = spread_products(late, range(late + 1))
+        held = []
+        gained = None
+        for other in range(tile + 1):
+            for step in range(LANES // 16):
+                form(other * LANES + step * 16, tile, other == tile)
+            if tile not in range(tiles - 2, tiles - 1):
+                gained = spread_products(tile, [other], gained)
+        if tile in range(tiles - 2, tiles - 1):
+            held.append(tile)
+        else:
+            image[:, lanes_of((tile, tile + 1))] = gained
 
     square_parts = fold(noise_full[...] * noise_full[...])
     inverse = 1.0 / (total(square_parts) + 1e-06)

time: 12.4 us -> 12.3 us (level)
    pallas_call x1, Pallas kernels: 11.6 us -> 11.5 us  [replicated(): pl.pallas_call(functools.partial(replicated_kernel, rows, cols), out_shap...]
where the time goes in v6:
time: 12.3 us; the launch traced here: 12.1 us
  Pallas kernels  11.5 us (93%)
  local copies, waits for them, and re-layouts  0.61 us (5%)
    pallas_call x1, Pallas kernels, replicated(): pl.pallas_call(functools.partial(replicated_kernel, rows, cols), out_shap...  11.5 us
    unnamed x1, local copies, waits for them, and re-layouts  0.61 us

profile of v6, /device:TPU:0, one launch (start us, length us, event | category | flops | bytes accessed | tf_op | source)
XLA Modules:
  0.0 12.1 jit_solution(5764156017672803361)
XLA Ops:
  0.0 11.5 %lanczos.1 = f32[3,16,32]{2,1,0:T(8,128)S(1)} custom-call(f32[3,16,32]{2,1,0:T(8,128)} %bitcast.3, f32[3,16]{1,0:T(4,128)} %pos_hbm.1), custom_call_target="tpu_custom_call" | custom-call | tf_op jit(solution)/shard_map/lanczos/pallas_call | solution.py:360
  11.5 0.6 %copy.4 = f32[32,3,16]{0,2,1:T(8,128)} copy(f32[32,3,16]{0,2,1:T(8,128)S(1)} %bitcast.2) | data formatting | bytes 12288

commit v7 on v6

--- a/solution.py
+++ b/solution.py
@@ -8,6 +8,7 @@
 from jax.sharding import PartitionSpec as P
 
 LANES = 128
+SHARED = 2
 LOGICAL = pl.DeviceIdType.LOGICAL
 BLOCKS = ((0, 0), (1, 1), (2, 2), (0, 1), (0, 2), (1, 2))
 
@@ -137,7 +138,7 @@
         def _(code=code):
             for target in both(code):
                 pl.semaphore_signal(
-                    grant.at[code], inc=1, device_id=target, device_id_type=LOGICAL
+                    grant.at[place[code] // SHARED], inc=1, device_id=target, device_id_type=LOGICAL
                 )
 
     for code in order[:0:-1]:
@@ -149,12 +150,21 @@
 
     send(0, 1, me + mate)
 
-    def send_later(code):
-        @pl.when(ahead[code] > 0)
+    def send_later(group):
+        codes = [code for code in order[group * SHARED : (group + 1) * SHARED] if code]
+        owed = 0
+        for code in codes:
+            owed = owed + jnp.where(ahead[code] > 0, 2, 0)
+
+        @pl.when(owed > 0)
         def _():
-            pl.semaphore_wait(grant.at[code], 2)
-            for side, target in enumerate(both(code)):
-                send(place[code], side, target)
+            pl.semaphore_wait(grant.at[group], owed)
+            for code in codes:
+
+                @pl.when(ahead[code] > 0)
+                def _(code=code):
+                    for side, target in enumerate(both(code)):
+                        send(place[code], side, target)
 
     lane = lax.broadcasted_iota(jnp.int32, (1, LANES), 1)
     field = lax.broadcasted_iota(jnp.int32, (LANES, 3 * LANES), 0) - 3 * samples
@@ -281,8 +291,8 @@
         if tile == 0:
             noise_full[:, pl.ds(0, per_device)] = own_turned[:fields]
 
-    for code in order[1:]:
-        send_later(code)
+    for group in range(chips // SHARED):
+        send_later(group)
     def spread_products(tile, others, gained=None):
         for other in others:
             part = onto_wide(noise_pieces((other, other + 1)), (other, other + 1), tile)
@@ -377,7 +387,7 @@
             pltpu.SemaphoreType.DMA((2,)),
             pltpu.SemaphoreType.DMA((1,)),
             pltpu.SemaphoreType.DMA((particles // LANES,)),
-            pltpu.SemaphoreType.REGULAR((chips,)),
+            pltpu.SemaphoreType.REGULAR((chips // SHARED,)),
         ],
         compiler_params=pltpu.CompilerParams(collective_id=0, has_side_effects=True),
         name="lanczos",

time: 12.3 us -> 12.2 us (level)
  no operation moved by 1% of the time
where the time goes in v7:
time: 12.2 us; the launch traced here: 12 us
  Pallas kernels  11.4 us (93%)
  local copies, waits for them, and re-layouts  0.61 us (5%)
    pallas_call x1, Pallas kernels, replicated(): pl.pallas_call(functools.partial(replicated_kernel, rows, cols), out_shap...  11.4 us
    unnamed x1, local copies, waits for them, and re-layouts  0.61 us

profile of v7, /device:TPU:0, one launch (start us, length us, event | category | flops | bytes accessed | tf_op | source)
XLA Modules:
  0.0 12.0 jit_solution(6998087450537823655)
XLA Ops:
  0.0 11.4 %lanczos.1 = f32[3,16,32]{2,1,0:T(8,128)S(1)} custom-call(f32[3,16,32]{2,1,0:T(8,128)} %bitcast.3, f32[3,16]{1,0:T(4,128)} %pos_hbm.1), custom_call_target="tpu_custom_call" | custom-call | tf_op jit(solution)/shard_map/lanczos/pallas_call | solution.py:370
  11.4 0.6 %copy.4 = f32[32,3,16]{0,2,1:T(8,128)} copy(f32[32,3,16]{0,2,1:T(8,128)S(1)} %bitcast.2) | data formatting | bytes 12288

commit v8 on v7

--- a/solution.py
+++ b/solution.py
@@ -66,7 +66,7 @@
     my_code = 0
     device, ahead, level = {0: me}, {0: 0}, {0: 0}
     for index, (weight, height) in enumerate(bits):
-        step = 18 if 2 <= weight < cols else 20
+        step = 19 if 2 <= weight < cols else 20
         height = height * step * chips + (1 << index)
         digit = lax.rem(me // weight, 2)
         my_code = my_code + (digit << index)

time: 12.2 us -> 12.2 us (level)
  no operation moved by 1% of the time
where the time goes in v8:
time: 12.2 us; the launch traced here: 12 us
  Pallas kernels  11.4 us (93%)
  local copies, waits for them, and re-layouts  0.61 us (5%)
    pallas_call x1, Pallas kernels, replicated(): pl.pallas_call(functools.partial(replicated_kernel, rows, cols), out_shap...  11.4 us
    unnamed x1, local copies, waits for them, and re-layouts  0.61 us

profile of v8, /device:TPU:0, one launch (start us, length us, event | category | flops | bytes accessed | tf_op | source)
XLA Modules:
  0.0 12.0 jit_solution(10705923673475604436)
XLA Ops:
  0.0 11.4 %lanczos.1 = f32[3,16,32]{2,1,0:T(8,128)S(1)} custom-call(f32[3,16,32]{2,1,0:T(8,128)} %bitcast.3, f32[3,16]{1,0:T(4,128)} %pos_hbm.1), custom_call_target="tpu_custom_call" | custom-call | tf_op jit(solution)/shard_map/lanczos/pallas_call | solution.py:370
  11.4 0.6 %copy.4 = f32[32,3,16]{0,2,1:T(8,128)} copy(f32[32,3,16]{0,2,1:T(8,128)S(1)} %bitcast.2) | data formatting | bytes 12288
